TPU v7x, 256 devices: a whole 4x4x8 slice. The times are simulated.
256 devices in a mesh: seq: 4 (over x_lo, core), dp: 64 (over x_hi, y, z).
Axes of the slice: x: 4 (x_hi: 2, x_lo: 2; x = x_hi * 2 + x_lo), y: 4, z: 8, core: 2. Of those that a mesh axis runs over, the one named last changes fastest.
Arguments:
- residual: bfloat16 [49152, 2560], P(('seq', 'dp')), may hold values from -6 to 6
- query_raw: bfloat16 [49152, 2560], P(('seq', 'dp')), may hold values from -60 to 60
- key_raw: bfloat16 [49152, 2560], P(('seq', 'dp')), may hold values from -60 to 60
- values: bfloat16 [49152, 2560], P(('seq', 'dp')), may hold values from -6 to 6
- residual_grad: bfloat16 [49152, 2560], P(('seq', 'dp')), may hold values from -6 to 6
- modulated_grad: bfloat16 [49152, 2560], P(('seq', 'dp')), may hold values from -24 to 24
- condition: float32 [64, 2, 2560], P('dp'), may hold values from -3 to 3
- modulation: float32 [2, 2560], P(None, ('seq', 'dp')), may hold values from -0.5 to 0.5
- norm_gains: float32 [2, 2560], P(None, ('seq', 'dp')), may hold values from 0.25 to 1.75
Outputs:
- input_grad: bfloat16 [49152, 2560], P(('seq', 'dp'))
- query_grad: bfloat16 [49152, 2560], P(('seq', 'dp'))
- key_grad: bfloat16 [49152, 2560], P(('seq', 'dp'))
- value_grad: bfloat16 [49152, 2560], P(('seq', 'dp'))
- param_grads: float32 [5, 2560], P(None, ('seq', 'dp'))
All inputs are finite; a program needn't handle non-finite values.
Results may differ from a plain program's by a relative error of at most 0.009.
The roundings to bfloat16 on the way count: a program that leaves them out, or rounds other values in their place, can miss the bound.
Values may be sent and summed in bfloat16 or wider, within the bound.
A program may use at most 128 MiB of HBM per device.

v0:
```python
import jax
import jax.numpy as jnp
from jax import lax
from jax.sharding import PartitionSpec as P

HEAD_DIM = 128
epsilon = 1e-06


def root_scale(raw_values):
    floats = raw_values.astype(jnp.float32)
    return lax.rsqrt(jnp.mean(floats * floats, axis=1, keepdims=True) + epsilon)


def head_scores(query_head, key_head):
    return lax.dot_general(
        query_head, key_head, (((1,), (1,)), ((), ())), preferred_element_type=jnp.float32
    ) * query_head.shape[-1] ** (-0.5)


def head_forward(pieces):
    query_head, key_head, value_head = pieces
    scores = head_scores(query_head, key_head)
    row_max = jnp.max(scores, axis=1, keepdims=True)
    row_sum = jnp.sum(jnp.exp(scores - row_max), axis=1, keepdims=True)
    logsum = row_max + jnp.log(row_sum)
    weights_low = jnp.exp(scores - logsum).astype(jnp.bfloat16)
    attended = jnp.dot(weights_low, value_head, preferred_element_type=jnp.float32).astype(
        jnp.bfloat16
    )
    return (attended, logsum[:, 0])


def head_backward(pieces):
    query_head, key_head, value_head, attended, attended_grad, logsum = pieces
    scores = head_scores(query_head, key_head)
    weights = jnp.exp(scores - logsum[:, None])
    row_dot = jnp.sum(
        attended_grad.astype(jnp.float32) * attended.astype(jnp.float32), axis=1, keepdims=True
    )
    weight_grad = lax.dot_general(
        attended_grad, value_head, (((1,), (1,)), ((), ())), preferred_element_type=jnp.float32
    )
    score_grad = (weights * (weight_grad - row_dot) * query_head.shape[-1] ** (-0.5)).astype(
        jnp.bfloat16
    )
    value_part = lax.dot_general(
        weights.astype(jnp.bfloat16),
        attended_grad,
        (((0,), (0,)), ((), ())),
        preferred_element_type=jnp.float32,
    )
    query_part = jnp.dot(score_grad, key_head, preferred_element_type=jnp.float32)
    key_part = lax.dot_general(
        score_grad, query_head, (((0,), (0,)), ((), ())), preferred_element_type=jnp.float32
    )
    return (query_part, key_part, value_part)


def stream_pass(residual, attended, modulated, residual_grad, modulated_grad):
    gate_row = modulated[0]
    scale_row = modulated[1]
    summed = residual.astype(jnp.float32) + gate_row * attended.astype(jnp.float32)
    centered = summed - jnp.mean(summed, axis=1, keepdims=True)
    norm_scale = lax.rsqrt(jnp.mean(centered * centered, axis=1, keepdims=True) + epsilon)
    normed = centered * norm_scale
    scaled_grad = modulated_grad.astype(jnp.float32) * (1.0 + scale_row)
    stream_grad = residual_grad.astype(jnp.float32) + norm_scale * (
        scaled_grad
        - jnp.mean(scaled_grad, axis=1, keepdims=True)
        - normed * jnp.mean(scaled_grad * normed, axis=1, keepdims=True)
    )
    attended_grad = (stream_grad * gate_row).astype(jnp.bfloat16)
    return (stream_grad, normed, attended_grad)


def norm_backward(raw_values, inverse, gain_row, upstream):
    floats = raw_values.astype(jnp.float32)
    weighted = gain_row * upstream
    return (
        inverse * weighted
        - floats * inverse**3 * jnp.mean(floats * weighted, axis=1, keepdims=True)
    ).astype(jnp.bfloat16)


def partial_sums(
    attended,
    stream_grad,
    normed,
    modulated_grad,
    query_raw,
    query_scale,
    query_part,
    key_raw,
    key_scale,
    key_part,
):
    grad_floats = modulated_grad.astype(jnp.float32)
    return jnp.stack(
        [
            jnp.sum(stream_grad * attended.astype(jnp.float32), axis=0),
            jnp.sum(grad_floats, axis=0),
            jnp.sum(grad_floats * normed, axis=0),
            jnp.sum(query_part * query_raw.astype(jnp.float32) * query_scale, axis=0),
            jnp.sum(key_part * key_raw.astype(jnp.float32) * key_scale, axis=0),
        ]
    )


def per_device(
    residual,
    query_raw,
    key_raw,
    values,
    residual_grad,
    modulated_grad,
    condition,
    modulation,
    norm_gains,
):
    head_width = HEAD_DIM
    row_count = residual.shape[0]
    modulation_all, gains_all = (
        lax.all_gather(modulation, ("seq", "dp"), axis=1, tiled=True),
        lax.all_gather(norm_gains, ("seq", "dp"), axis=1, tiled=True),
    )
    modulated = modulation_all + condition[0]
    query_scale = root_scale(query_raw)
    key_scale = root_scale(key_raw)
    normed_query = (query_raw.astype(jnp.float32) * query_scale * gains_all[0]).astype(jnp.bfloat16)
    normed_key = (key_raw.astype(jnp.float32) * key_scale * gains_all[1]).astype(jnp.bfloat16)
    query_moved, key_moved, value_moved = (
        lax.all_to_all(
            normed_query.reshape(row_count, -1, head_width),
            "seq",
            split_axis=1,
            concat_axis=0,
            tiled=True,
        ),
        lax.all_to_all(
            normed_key.reshape(row_count, -1, head_width),
            "seq",
            split_axis=1,
            concat_axis=0,
            tiled=True,
        ),
        lax.all_to_all(
            values.reshape(row_count, -1, head_width),
            "seq",
            split_axis=1,
            concat_axis=0,
            tiled=True,
        ),
    )
    query_heads = query_moved.transpose(1, 0, 2)
    key_heads = key_moved.transpose(1, 0, 2)
    value_heads = value_moved.transpose(1, 0, 2)
    attended_heads, logsum = lax.map(head_forward, (query_heads, key_heads, value_heads))
    attended_tokens = lax.all_to_all(
        attended_heads.transpose(1, 0, 2), "seq", split_axis=0, concat_axis=1, tiled=True
    )
    attended = attended_tokens.reshape(row_count, -1)
    stream_grad, normed, attended_grad = stream_pass(
        residual, attended, modulated, residual_grad, modulated_grad
    )
    grad_moved = lax.all_to_all(
        attended_grad.reshape(row_count, -1, head_width),
        "seq",
        split_axis=1,
        concat_axis=0,
        tiled=True,
    )
    query_part, key_part, value_part = lax.map(
        head_backward,
        (
            query_heads,
            key_heads,
            value_heads,
            attended_heads,
            grad_moved.transpose(1, 0, 2),
            logsum,
        ),
    )
    query_back, key_back, value_back = (
        lax.all_to_all(
            query_part.transpose(1, 0, 2), "seq", split_axis=0, concat_axis=1, tiled=True
        ),
        lax.all_to_all(key_part.transpose(1, 0, 2), "seq", split_axis=0, concat_axis=1, tiled=True),
        lax.all_to_all(
            value_part.transpose(1, 0, 2), "seq", split_axis=0, concat_axis=1, tiled=True
        ),
    )
    query_grad_n = query_back.reshape(row_count, -1)
    key_grad_n = key_back.reshape(row_count, -1)
    value_sum = value_back.reshape(row_count, -1)
    sums_here = partial_sums(
        attended,
        stream_grad,
        normed,
        modulated_grad,
        query_raw,
        query_scale,
        query_grad_n,
        key_raw,
        key_scale,
        key_grad_n,
    )
    reduced = lax.psum_scatter(sums_here, ("seq", "dp"), scatter_dimension=1, tiled=True)
    factor = (row_count * lax.axis_size("seq") * lax.axis_size("dp")) ** (-0.5)
    return (
        stream_grad.astype(jnp.bfloat16),
        norm_backward(query_raw, query_scale, gains_all[0], query_grad_n),
        norm_backward(key_raw, key_scale, gains_all[1], key_grad_n),
        value_sum.astype(jnp.bfloat16),
        reduced * factor,
    )


def solution(mesh):
    placed = (
        P(("seq", "dp"), None),
        P(("seq", "dp"), None),
        P(("seq", "dp"), None),
        P(("seq", "dp"), None),
        P(("seq", "dp"), None),
        P(("seq", "dp"), None),
        P("dp", None, None),
        P(None, ("seq", "dp")),
        P(None, ("seq", "dp")),
    )
    return jax.shard_map(
        per_device,
        mesh=mesh,
        in_specs=placed,
        out_specs=(
            P(("seq", "dp"), None),
            P(("seq", "dp"), None),
            P(("seq", "dp"), None),
            P(("seq", "dp"), None),
            P(None, ("seq", "dp")),
        ),
        check_vma=False,
    )
```

profile of v0, /device:TPU:1, one launch (start us, length us, event | category | flops | bytes accessed | tf_op | source)
XLA Modules:
  0.0 1958.0 jit_solution(11873094181766818667)
XLA Ops:
  3.0 6.7 all-to-all-start.2
  9.8 647.2 %all-gather.1 = f32[256,10,2]{1,2,0:T(2,128)S(1)} all-gather(f32[1,10,2]{1,2,0:T(2,128)S(1)} %bitcast.194), channel_id=1, replica_groups=mesh['seq'=4,'dp'=64] {'seq','dp'}, dimensions={0}, use_global_device_ids=true | all-gather | bytes 20560 | tf_op jit(solution)/shard_map/all_gather | solution.py:125
  669.4 4.2 all-to-all-start.1
  675.9 10.5 all-to-all-done.1
  686.4 5.1 all-to-all-start
  691.5 664.9 %all-gather = f32[256,10,2]{1,2,0:T(2,128)S(1)} all-gather(f32[1,10,2]{1,2,0:T(2,128)S(1)} %bitcast.195), channel_id=1, replica_groups=mesh['seq'=4,'dp'=64] {'seq','dp'}, dimensions={0}, use_global_device_ids=true | all-gather | bytes 20560 | tf_op jit(solution)/shard_map/all_gather | solution.py:124
  1368.5 27.5 %while.26 = (s32[]{:T(128)}, bf16[5,768,128]{2,1,0:T(8,128)(2,1)}, f32[5,768]{1,0:T(8,128)}, bf16[5,768,128]{2,1,0:T(8,128)(2,1)}, bf16[5,768,128]{2,1,0:T(8,128...) while((s32[]{:T(128)}, bf16[5,768,128]{2,1,0:T(8,128)(2,1)}, f32[5,768]{1,0:T(8,128)}, ...), condition=%wide.region_5.6_spmd, body=%wide.region_2.5_spmd.sunk | while | flops 306806016 | bytes 7900257 | solution.py:158
  1399.1 4.7 all-to-all-start.3
  1403.9 19.2 all-to-all-done.3
  1438.7 4.3 all-to-all-start.4
  1443.0 12.9 all-to-all-done.4
  1457.1 218.5 %while.27 = (s32[]{:T(128)}, f32[5,768,128]{2,0,1:T(8,128)}, f32[5,768,128]{2,0,1:T(8,128)}, bf16[5,768,128]{2,0,1:T(8,128)(2,1)}, bf16[5,768,128]{2,1,0:T(8,128...) while((s32[]{:T(128)}, f32[5,768,128]{2,0,1:T(8,128)}, ...), condition=%wide.region_12.13_spmd, body=%wide.region_10.12_spmd.sunk | while | flops 760675584 | bytes 15945885 | solution.py:173
  1466.9 11.0 dynamic_update_slice.28
  1477.9 11.4 dynamic_update_slice.27
  1489.3 11.4 dynamic_update_slice.26
  1510.6 11.0 dynamic_update_slice.28
  1521.6 11.4 dynamic_update_slice.27
  1533.0 11.4 dynamic_update_slice.26
  1554.3 11.0 dynamic_update_slice.28
  1565.3 11.4 dynamic_update_slice.27
  1576.7 11.4 dynamic_update_slice.26
  1598.0 11.0 dynamic_update_slice.28
  1609.0 11.4 dynamic_update_slice.27
  1620.4 11.4 dynamic_update_slice.26
  1641.7 11.0 dynamic_update_slice.28
  1652.7 11.4 dynamic_update_slice.27
  1664.1 11.4 dynamic_update_slice.26
  1675.5 24.6 %all_to_all.120 = bf16[768,5,128]{2,1,0:T(8,128)(2,1)} all-to-all(bf16[768,5,128]{2,1,0:T(8,128)(2,1)} %bitcast.192), channel_id=1, replica_groups=mesh['seq'=4,'dp'=64] {'seq'}, dimensions={0} | all-to-all | bytes 1966080 | tf_op jit(solution)/shard_map/all_to_all | solution.py:189
  1700.1 40.3 %all_to_all.121 = f32[768,5,128]{2,1,0:T(8,128)} all-to-all(f32[768,5,128]{2,1,0:T(8,128)S(1)} %bitcast.191), channel_id=1, replica_groups=mesh['seq'=4,'dp'=64] {'seq'}, dimensions={0} | all-to-all | bytes 3932160 | tf_op jit(solution)/shard_map/all_to_all | solution.py:185
  1740.4 5.6 all-to-all-start.6
  1756.7 25.5 %all-to-all-done.6 = f32[768,5,128]{2,1,0:T(8,128)} async-done(((f32[768,5,128]{2,1,0:T(8,128)}), f32[768,5,128]{2,1,0:T(8,128)}, u32[]{:S(2)}, u32[]{:S(2)}) %all-to-all-start.6) | async-done | bytes 1966112 | tf_op jit(solution)/shard_map/all_to_all | solution.py:188
  1800.0 157.2 %all-reduce = f32[5,2560]{1,0:T(8,128)S(1)} all-reduce(f32[5,2560]{1,0:T(8,128)S(1)} %stack.23), channel_id=2, replica_groups=mesh['seq'=4,'dp'=64] {'seq','dp'}, use_global_device_ids=true, to_apply=%region_20.21.clone | all-reduce | flops 12800 | bytes 102400
  (168 shorter events, 154.7 us)
Async XLA Ops:
  0.6 1.2 copy-start
  0.6 9.1 copy-start.18
  0.7 656.6 %copy-start.9 = (bf16[192,2560]{1,0:T(8,128)(2,1)S(1)}, bf16[192,2560]{1,0:T(8,128)(2,1)}, u32[]{:S(2)}) copy-start(bf16[192,2560]{1,0:T(8,128)(2,1)} %param.14) | copy-start | bytes 2949124
  3.0 666.3 %all-to-all-start.2 = ((bf16[192,20,128]{2,0,1:T(8,128)(2,1)}), bf16[192,20,128]{2,0,1:T(8,128)(2,1)S(1)}, u32[]{:S(2)}, u32[]{:S(2)}) async-start(bf16[192,20,128]{2,0,1:T(8,128)(2,1)} %copy_bitcast_fusion.1), calls=%async_computation.2 | async-start | bytes 1966080 | tf_op jit(solution)/shard_map/all_to_all | solution.py:147
  657.2 6.3 copy-start.10
  663.5 3.5 copy-start.14
  669.4 17.1 all-to-all-start.1
  673.5 18.0 copy-start.19
  686.4 679.9 %all-to-all-start = ((bf16[192,20,128]{2,0,1:T(8,128)(2,1)}), bf16[192,20,128]{2,0,1:T(8,128)(2,1)}, u32[]{:S(2)}, u32[]{:S(2)}) async-start(bf16[192,20,128]{2,0,1:T(8,128)(2,1)} %copy.75), calls=%async_computation | async-start | bytes 1966080 | tf_op jit(solution)/shard_map/all_to_all | solution.py:133
  1396.0 7.8 copy-start.12
  1396.0 7.8 copy-start.13
  1399.1 24.0 %all-to-all-start.3 = ((bf16[768,5,128]{2,1,0:T(8,128)(2,1)}), bf16[768,5,128]{2,1,0:T(8,128)(2,1)}, u32[]{:S(2)}, u32[]{:S(2)}) async-start(bf16[768,5,128]{2,1,0:T(8,128)(2,1)} %bitcast.181), calls=%async_computation.3 | async-start | bytes 3145728 | tf_op jit(solution)/shard_map/all_to_all | solution.py:159
  1428.8 1.3 copy-start.6
  1429.2 3.0 copy-start.5
  1429.2 3.0 copy-start.7
  1438.7 17.2 all-to-all-start.4
  1675.5 24.6 %copy-start.8 = (f32[5,768,128]{2,0,1:T(8,128)S(1)}, f32[5,768,128]{2,0,1:T(8,128)}, u32[]{:S(2)}) copy-start(f32[5,768,128]{2,0,1:T(8,128)} %get-tuple-element.94) | copy-start | bytes 5898244
  1740.4 41.8 %all-to-all-start.6 = ((f32[768,5,128]{2,1,0:T(8,128)}), f32[768,5,128]{2,1,0:T(8,128)}, u32[]{:S(2)}, u32[]{:S(2)}) async-start(f32[768,5,128]{2,1,0:T(8,128)} %bitcast.190), calls=%async_computation.6 | async-start | bytes 6291456 | tf_op jit(solution)/shard_map/all_to_all | solution.py:188
  1782.2 3.4 copy-start.11
  1782.2 3.4 copy-start.15
  1785.6 3.4 copy-start.2
  1785.6 3.4 copy-start.4
  1785.6 3.4 copy-start.17
  1790.6 5.3 copy-start.16
  1793.0 3.0 copy-start.3
  1795.9 162.0 %copy-start.1 = (bf16[192,2560]{1,0:T(8,128)(2,1)S(1)}, bf16[192,2560]{1,0:T(8,128)(2,1)}, u32[]{:S(2)}) copy-start(bf16[192,2560]{1,0:T(8,128)(2,1)} %param.16) | copy-start | bytes 2949124
where the time goes:
time: 1960 us
  blocking collectives  1530 us (78%)
  local copies, waits for them, and re-layouts  232 us (12%)
  waiting for transfers between devices  68.1 us (3%)
  matrix products  57.8 us (3%)
  other arithmetic  34.3 us (2%)
  starting transfers between devices  30.7 us (2%)
    all_gather x1, blocking collectives, per_device(): lax.all_gather(modulation, ('seq', 'dp'), axis=1, tiled=True)  665 us
    all_gather x1, blocking collectives, per_device(): lax.all_gather(norm_gains, ('seq', 'dp'), axis=1, tiled=True)  647 us
    dynamic_update_slice x15, local copies, waits for them, and re-layouts, per_device(): lax.map(head_backward, (query_heads, key_heads, value_heads, attended_hea...  169 us
    unnamed x1, blocking collectives  157 us
    all_to_all x1, blocking collectives, per_device(): lax.all_to_all(query_part.transpose(1, 0, 2), 'seq', split_axis=0, concat...  40.3 us
  transfers between devices with their start and end apart: 6, of which 4 were waited for; matrix products, arithmetic and copies ran while one was open for 2% of the time, Pallas kernels for 0%

commit v1 on v0

--- a/solution.py
+++ b/solution.py
@@ -5,6 +5,12 @@
 
 HEAD_DIM = 128
 epsilon = 1e-06
+
+
+def swap_blocks(block, mesh_axis, split, join):
+    pieces = jnp.split(block, lax.axis_size(mesh_axis), axis=split)
+    received = lax.all_to_all(jnp.stack(pieces), mesh_axis, 0, 0)
+    return jnp.concatenate(received, axis=join)
 
 
 def root_scale(raw_values):
@@ -182,9 +188,7 @@
         ),
     )
     query_back, key_back, value_back = (
-        lax.all_to_all(
-            query_part.transpose(1, 0, 2), "seq", split_axis=0, concat_axis=1, tiled=True
-        ),
+        swap_blocks(query_part.transpose(1, 0, 2), "seq", 0, 1),
         lax.all_to_all(key_part.transpose(1, 0, 2), "seq", split_axis=0, concat_axis=1, tiled=True),
         lax.all_to_all(
             value_part.transpose(1, 0, 2), "seq", split_axis=0, concat_axis=1, tiled=True

time: 1960 us -> 1880 us (0.959)
  local copies, waits for them, and re-layouts: 232 us -> 175 us
  blocking collectives: 1530 us -> 1490 us
    dynamic_update_slice x15 -> x10, local copies, waits for them, and re-layouts: 169 us -> 112 us  [per_device(): lax.map(head_backward, (query_heads, key_heads, value_heads, attended_hea...]
    all_to_all x1 -> x0, blocking collectives: 40.3 us -> none  [per_device(): lax.all_to_all(query_part.transpose(1, 0, 2), 'seq', split_axis=0, concat...]
  transfers between devices with their start and end apart: 6 -> 7, of which waited for: 4 -> 5; matrix products, arithmetic and copies ran while one was open for 2% -> 2% of each run, Pallas kernels for 0% -> 0%
where the time goes in v1:
time: 1880 us
  blocking collectives  1490 us (79%)
  local copies, waits for them, and re-layouts  175 us (9%)
  waiting for transfers between devices  81.1 us (4%)
  matrix products  56.5 us (3%)
  starting transfers between devices  36 us (2%)
  other arithmetic  35.2 us (2%)
    all_gather x1, blocking collectives, per_device(): lax.all_gather(modulation, ('seq', 'dp'), axis=1, tiled=True)  665 us
    all_gather x1, blocking collectives, per_device(): lax.all_gather(norm_gains, ('seq', 'dp'), axis=1, tiled=True)  647 us
    unnamed x1, blocking collectives  157 us
    dynamic_update_slice x10, local copies, waits for them, and re-layouts, per_device(): lax.map(head_backward, (query_heads, key_heads, value_heads, attended_hea...  112 us
  transfers between devices with their start and end apart: 7, of which 5 were waited for; matrix products, arithmetic and copies ran while one was open for 2% of the time, Pallas kernels for 0%

profile of v1, /device:TPU:1, one launch (start us, length us, event | category | flops | bytes accessed | tf_op | source)
XLA Modules:
  0.0 1878.6 jit_solution(9503832808242437518)
XLA Ops:
  3.0 6.7 all-to-all-start.2
  9.8 647.2 %all-gather.1 = f32[256,10,2]{1,2,0:T(2,128)S(1)} all-gather(f32[1,10,2]{1,2,0:T(2,128)S(1)} %bitcast.199), channel_id=1, replica_groups=mesh['seq'=4,'dp'=64] {'seq','dp'}, dimensions={0}, use_global_device_ids=true | all-gather | bytes 20560 | tf_op jit(solution)/shard_map/all_gather | solution.py:131
  663.5 3.5 fusion.55
  669.3 4.2 all-to-all-start.1
  675.9 10.5 all-to-all-done.1
  686.4 5.1 all-to-all-start
  691.5 664.9 %all-gather = f32[256,10,2]{1,2,0:T(2,128)S(1)} all-gather(f32[1,10,2]{1,2,0:T(2,128)S(1)} %bitcast.200), channel_id=1, replica_groups=mesh['seq'=4,'dp'=64] {'seq','dp'}, dimensions={0}, use_global_device_ids=true | all-gather | bytes 20560 | tf_op jit(solution)/shard_map/all_gather | solution.py:130
  1368.5 27.5 %while.26 = (s32[]{:T(128)}, bf16[5,768,128]{2,1,0:T(8,128)(2,1)}, f32[5,768]{1,0:T(8,128)}, bf16[5,768,128]{2,1,0:T(8,128)(2,1)}, bf16[5,768,128]{2,1,0:T(8,128...) while((s32[]{:T(128)}, bf16[5,768,128]{2,1,0:T(8,128)(2,1)}, f32[5,768]{1,0:T(8,128)}, ...), condition=%wide.region_5.6_spmd, body=%wide.region_2.5_spmd.sunk | while | flops 306806016 | bytes 7900257 | solution.py:164
  1396.0 3.1 copy.126
  1399.1 4.7 all-to-all-start.3
  1403.9 19.2 %all-to-all-done.3 = bf16[768,5,128]{2,1,0:T(8,128)(2,1)} async-done(((bf16[768,5,128]{2,1,0:T(8,128)(2,1)}), bf16[768,5,128]{2,1,0:T(8,128)(2,1)}, u32[]{:S(2)}, u32[]{:S(2)}) %all-to-all-start.3) | async-done | bytes 983072 | tf_op jit(solution)/shard_map/all_to_all | solution.py:165
  1438.6 4.3 all-to-all-start.4
  1442.9 12.9 all-to-all-done.4
  1455.9 159.6 %while.27 = (s32[]{:T(128)}, f32[5,768,128]{2,1,0:T(8,128)}, f32[5,768,128]{2,0,1:T(8,128)}, bf16[5,768,128]{2,0,1:T(8,128)(2,1)}, bf16[5,768,128]{2,1,0:T(8,128...) while((s32[]{:T(128)}, f32[5,768,128]{2,1,0:T(8,128)}, ...), condition=%wide.region_12.13_spmd, body=%wide.region_10.12_spmd.sunk | while | flops 760675584 | bytes 15163541 | solution.py:179
  1465.4 11.0 dynamic_update_slice.29
  1476.4 11.4 dynamic_update_slice.28
  1497.4 11.0 dynamic_update_slice.29
  1508.3 11.4 dynamic_update_slice.28
  1529.3 11.0 dynamic_update_slice.29
  1540.3 11.4 dynamic_update_slice.28
  1561.2 11.0 dynamic_update_slice.29
  1572.2 11.4 dynamic_update_slice.28
  1593.1 11.0 dynamic_update_slice.29
  1604.1 11.4 dynamic_update_slice.28
  1615.5 24.3 %all_to_all.110 = bf16[768,5,128]{2,1,0:T(8,128)(2,1)} all-to-all(bf16[768,5,128]{2,1,0:T(8,128)(2,1)} %bitcast.197), channel_id=1, replica_groups=mesh['seq'=4,'dp'=64] {'seq'}, dimensions={0} | all-to-all | bytes 1966080 | tf_op jit(solution)/shard_map/all_to_all | solution.py:193
  1639.8 5.7 all-to-all-start.6
  1648.7 33.0 %all-to-all-done.6 = f32[768,5,128]{2,1,0:T(8,128)} async-done(((f32[768,5,128]{2,1,0:T(8,128)}), f32[768,5,128]{2,1,0:T(8,128)}, u32[]{:S(2)}, u32[]{:S(2)}) %all-to-all-start.6) | async-done | bytes 1966112 | tf_op jit(solution)/shard_map/all_to_all | solution.py:192
  1681.7 5.3 all-to-all-start.5
  1694.3 3.4 copy.91
  1697.8 3.3 fusion.70
  1705.1 5.4 all-to-all-done.5
  1720.7 157.3 %all-reduce = f32[5,2560]{1,0:T(8,128)S(1)} all-reduce(f32[5,2560]{1,0:T(8,128)S(1)} %stack.43), channel_id=2, replica_groups=mesh['seq'=4,'dp'=64] {'seq','dp'}, use_global_device_ids=true, to_apply=%region_20.21.clone | all-reduce | flops 12800 | bytes 102400
  (164 shorter events, 141.4 us)
Async XLA Ops:
  0.6 1.2 copy-start
  0.6 9.1 copy-start.17
  0.7 656.6 %copy-start.8 = (bf16[192,2560]{1,0:T(8,128)(2,1)S(1)}, bf16[192,2560]{1,0:T(8,128)(2,1)}, u32[]{:S(2)}) copy-start(bf16[192,2560]{1,0:T(8,128)(2,1)} %param.14) | copy-start | bytes 2949124
  3.0 666.3 %all-to-all-start.2 = ((bf16[192,20,128]{2,0,1:T(8,128)(2,1)}), bf16[192,20,128]{2,0,1:T(8,128)(2,1)S(1)}, u32[]{:S(2)}, u32[]{:S(2)}) async-start(bf16[192,20,128]{2,0,1:T(8,128)(2,1)} %copy_bitcast_fusion.1), calls=%async_computation.2 | async-start | bytes 1966080 | tf_op jit(solution)/shard_map/all_to_all | solution.py:153
  657.2 6.2 copy-start.9
  663.5 3.5 copy-start.13
  669.3 17.1 all-to-all-start.1
  673.5 18.0 copy-start.18
  686.4 679.9 %all-to-all-start = ((bf16[192,20,128]{2,0,1:T(8,128)(2,1)}), bf16[192,20,128]{2,0,1:T(8,128)(2,1)}, u32[]{:S(2)}, u32[]{:S(2)}) async-start(bf16[192,20,128]{2,0,1:T(8,128)(2,1)} %copy.75), calls=%async_computation | async-start | bytes 1966080 | tf_op jit(solution)/shard_map/all_to_all | solution.py:139
  1396.0 7.9 copy-start.11
  1396.0 7.9 copy-start.12
  1399.1 24.1 %all-to-all-start.3 = ((bf16[768,5,128]{2,1,0:T(8,128)(2,1)}), bf16[768,5,128]{2,1,0:T(8,128)(2,1)}, u32[]{:S(2)}, u32[]{:S(2)}) async-start(bf16[768,5,128]{2,1,0:T(8,128)(2,1)} %bitcast.187), calls=%async_computation.3 | async-start | bytes 3145728 | tf_op jit(solution)/shard_map/all_to_all | solution.py:165
  1428.8 1.3 copy-start.6
  1429.2 3.0 copy-start.5
  1429.2 3.0 copy-start.7
  1438.6 17.2 all-to-all-start.4
  1639.8 41.9 %all-to-all-start.6 = ((f32[768,5,128]{2,1,0:T(8,128)}), f32[768,5,128]{2,1,0:T(8,128)}, u32[]{:S(2)}, u32[]{:S(2)}) async-start(f32[768,5,128]{2,1,0:T(8,128)} %bitcast.196), calls=%async_computation.6 | async-start | bytes 6291456 | tf_op jit(solution)/shard_map/all_to_all | solution.py:192
  1681.7 28.8 %all-to-all-start.5 = ((f32[4,192,5,128]{3,1,2,0:T(8,128)}), f32[4,192,5,128]{3,1,2,0:T(8,128)}, u32[]{:S(2)}, u32[]{:S(2)}) async-start(f32[4,192,5,128]{3,1,2,0:T(8,128)} %pad_maximum_fusion), calls=%async_computation.5 | async-start | bytes 3932160 | tf_op jit(solution)/shard_map/all_to_all | solution.py:12
  1694.3 3.4 copy-start.10
  1694.3 3.4 copy-start.14
  1697.7 3.4 copy-start.2
  1697.7 3.4 copy-start.3
  1697.8 3.4 copy-start.16
  1713.6 3.0 copy-start.4
  1713.6 3.0 copy-start.15
  1716.6 162.0 %copy-start.1 = (bf16[192,2560]{1,0:T(8,128)(2,1)S(1)}, bf16[192,2560]{1,0:T(8,128)(2,1)}, u32[]{:S(2)}) copy-start(bf16[192,2560]{1,0:T(8,128)(2,1)} %param.16) | copy-start | bytes 2949124
